TPU v7x, 256 devices: a whole 4x4x8 slice. The times are simulated.
256 devices in a mesh: chan: 16 (over y, x_hi, core), win: 16 (over z, x_lo).
Axes of the slice: x: 4 (x_hi: 2, x_lo: 2; x = x_hi * 2 + x_lo), y: 4, z: 8, core: 2. Of those that a mesh axis runs over, the one named last changes fastest.
Arguments:
- spectra: bfloat16 [64, 512, 4096], P('win', 'chan'), may hold values from -80 to 80
- quality: int32 [512], P('chan'), may hold values 0 or 1
- source_block: int32 [2], replicated, may hold values from 0 to 63
Outputs:
- correlations: bfloat16 [2, 512, 8, 512], P(None, ('chan', 'win'))
All inputs are finite; a program needn't handle non-finite values. No bound on the sum of `quality` on one device may be relied on, other than what follows from the above.
Results may differ from a plain program's by a relative error of at most 0.0045.
Values may be sent and summed in bfloat16 or wider, within the bound.
A program may use at most 192 MiB of HBM per device.

v0:
```python
import math
import jax
import jax.numpy as jnp
from jax import lax
from jax.sharding import PartitionSpec as P

L = 512
SRC = 8
STEPS = 2


def from_root(value, axis, source):
    kept = jnp.where(lax.axis_index(axis) == source, value, 0).astype(value.dtype)
    return lax.psum(kept, axis)


def lag_table(bins, lags, factor):
    bin_index = lax.iota(jnp.int32, bins)[:, None]
    shifts = lax.iota(jnp.int32, lags)[None, :] - lags // 2
    residue = jnp.mod(bin_index * shifts, 2 * bins)
    phase_angle = residue.astype(jnp.float32) * (2.0 * math.pi / (2 * bins))
    return jnp.concatenate([jnp.cos(phase_angle), -jnp.sin(phase_angle)], axis=0) * factor


def whiten(block, quality):
    values = block.astype(jnp.float32)
    bins = values.shape[-1] // 2
    energy = jnp.sum(values * values, axis=-1) / bins
    weights = quality.astype(jnp.float32)[None, :] / jnp.sqrt(energy + 1e-06)
    return (values * weights[:, :, None]).astype(jnp.bfloat16)


def cross_spectra(sources, receivers):
    bins = sources.shape[-1] // 2
    src_real = sources[:, :, :bins]
    src_imag = sources[:, :, bins:]
    rec_real = receivers[:, :, :bins]
    rec_imag = receivers[:, :, bins:]
    real_part = jnp.einsum("wsf,wrf->rsf", src_real, rec_real, preferred_element_type=jnp.float32)
    real_part = real_part + jnp.einsum(
        "wsf,wrf->rsf", src_imag, rec_imag, preferred_element_type=jnp.float32
    )
    imag_part = jnp.einsum("wsf,wrf->rsf", src_real, rec_imag, preferred_element_type=jnp.float32)
    imag_part = imag_part - jnp.einsum(
        "wsf,wrf->rsf", src_imag, rec_real, preferred_element_type=jnp.float32
    )
    return jnp.concatenate([real_part, imag_part], axis=-1)


def apply_lags(cross, transform):
    lagged = jnp.dot(
        cross.reshape(-1, cross.shape[-1]),
        transform,
        precision=lax.Precision.HIGHEST,
        preferred_element_type=jnp.float32,
    )
    return lagged.reshape(cross.shape[0], cross.shape[1], transform.shape[1])


def body(spectra, quality, source_block):
    window_count, channel_count, row_width = spectra.shape
    bins = row_width // 2
    total_windows = window_count * lax.axis_size("win")
    transform = lag_table(bins, L, 1.0 / math.sqrt(row_width * total_windows))
    whitened = whiten(spectra, quality)
    per_group = channel_count // SRC
    results = []
    for step in range(STEPS):
        block_index = source_block[step]
        root_group = block_index // per_group
        offset = block_index % per_group * SRC
        own_block = lax.dynamic_slice_in_dim(whitened, offset, SRC, 1)
        sources = from_root(own_block, "chan", root_group)
        partial_cross = cross_spectra(sources, whitened)
        stacked = lax.psum_scatter(partial_cross, "win", scatter_dimension=0, tiled=True)
        lagged = apply_lags(stacked, transform)
        results.append(lagged.astype(jnp.bfloat16))
    return jnp.stack(results)


def solution(mesh):
    return jax.shard_map(
        body,
        mesh=mesh,
        in_specs=(P("win", "chan", None), P("chan"), P()),
        out_specs=P(None, ("chan", "win"), None, None),
        check_vma=False,
    )
```

profile of v0, /device:TPU:8, one launch (start us, length us, event | category | flops | bytes accessed | tf_op | source)
XLA Modules:
  0.0 444.0 jit_solution(556799293227208969)
XLA Ops:
  13.1 1.5 fusion.13
  17.8 2.5 copy.4
  21.7 136.2 %all-reduce.3.cloned.1.call-done = (bf16[4,8,4096]{2,1,0:T(8,128)(2,1)}, bf16[4,8,4096]{2,1,0:T(8,128)(2,1)}) async-done(((bf16[4,8,4096]{2,1,0:T(8,128)(2,1)}, bf16[4,8,4096]{2,1,0:T(8,128)(2,1)}), (bf16[4,8,4096]{2,1,0:T(8,128)(2,1)}, bf16[4,8,4096]{2,1,0:T(8,128)(2,1)})) %all-reduce.3.cloned.1.call-update) | async-done | bytes 524304 | tf_op jit(solution)/shard_map/psum | solution.py:14
  159.0 2.4 copy.5
  161.5 2.4 copy.8
  163.9 7.4 %fusion.36 = f32[2048,32,8]{1,2,0:T(8,128)} fusion(bf16[4,32,2048]{1,0,2:T(4,128)(2,1)} %copy.4, bf16[4,8,2048]{1,0,2:T(4,128)(2,1)} %copy.5), kind=kOutput, calls=%fused_computation.44 | convolution fusion | flops 4194304 | bytes 2752512 | tf_op jit(solution)/shard_map/wsf,wrf->rsf/dot_general | solution.py:39
  171.3 4.8 %fusion.38 = f32[2048,32,8]{1,2,0:T(8,128)} fusion(bf16[4,32,2048]{1,0,2:T(4,128)(2,1)S(1)} %copy.7, bf16[4,8,2048]{1,0,2:T(4,128)(2,1)S(1)} %copy-done.2), kind=kOutput, calls=%fused_computation.46 | convolution fusion | flops 4194304 | bytes 2752512 | tf_op jit(solution)/shard_map/wsf,wrf->rsf/dot_general | solution.py:43
  176.1 4.8 %fusion.37 = f32[2048,32,8]{1,2,0:T(8,128)} fusion(bf16[4,32,2048]{1,0,2:T(4,128)(2,1)S(1)} %copy.7, bf16[4,8,2048]{1,0,2:T(4,128)(2,1)S(1)} %copy-done.1), kind=kOutput, calls=%fused_computation.45 | convolution fusion | flops 4194304 | bytes 2752512 | tf_op jit(solution)/shard_map/wsf,wrf->rsf/dot_general | solution.py:40
  180.9 4.8 %fusion.39 = f32[2048,32,8]{1,2,0:T(8,128)} fusion(bf16[4,32,2048]{1,0,2:T(4,128)(2,1)S(1)} %copy-done, bf16[4,8,2048]{1,0,2:T(4,128)(2,1)S(1)} %copy-done.1), kind=kOutput, calls=%fused_computation.47 | convolution fusion | flops 4194304 | bytes 2752512 | tf_op jit(solution)/shard_map/wsf,wrf->rsf/dot_general | solution.py:44
  185.7 6.7 %copy.6 = f32[2048,32,8]{0,2,1:T(8,128)} copy(f32[2048,32,8]{1,2,0:T(8,128)} %fusion.36) | data formatting | bytes 4194304 | tf_op jit(solution)/shard_map/wsf,wrf->rsf/dot_general | solution.py:39
  192.3 6.6 %copy.9 = f32[2048,32,8]{0,2,1:T(8,128)} copy(f32[2048,32,8]{1,2,0:T(8,128)} %fusion.37) | data formatting | bytes 4194304 | tf_op jit(solution)/shard_map/wsf,wrf->rsf/dot_general | solution.py:40
  198.9 6.6 %copy.10 = f32[2048,32,8]{0,2,1:T(8,128)} copy(f32[2048,32,8]{1,2,0:T(8,128)} %fusion.38) | data formatting | bytes 4194304 | tf_op jit(solution)/shard_map/wsf,wrf->rsf/dot_general | solution.py:43
  205.6 6.6 %copy.11 = f32[2048,32,8]{0,2,1:T(8,128)} copy(f32[2048,32,8]{1,2,0:T(8,128)} %fusion.39) | data formatting | bytes 4194304 | tf_op jit(solution)/shard_map/wsf,wrf->rsf/dot_general | solution.py:44
  212.2 2.7 add_bitcast_fusion.1
  215.9 2.4 pad_maximum_fusion
  218.6 2.5 copy.12
  221.1 7.2 %fusion.40 = f32[2048,32,8]{1,2,0:T(8,128)} fusion(bf16[4,32,2048]{1,0,2:T(4,128)(2,1)} %copy.4, bf16[4,8,2048]{1,0,2:T(4,128)(2,1)} %copy.12), kind=kOutput, calls=%fused_computation.48 | convolution fusion | flops 4194304 | bytes 2752512 | tf_op jit(solution)/shard_map/wsf,wrf->rsf/dot_general | solution.py:39
  228.3 6.6 %copy.13 = f32[2048,32,8]{0,2,1:T(8,128)} copy(f32[2048,32,8]{1,2,0:T(8,128)} %fusion.40) | data formatting | bytes 4194304 | tf_op jit(solution)/shard_map/wsf,wrf->rsf/dot_general | solution.py:39
  234.9 2.4 copy.14
  237.3 6.1 %fusion.41 = f32[2048,32,8]{1,2,0:T(8,128)} fusion(bf16[4,32,2048]{1,0,2:T(4,128)(2,1)S(1)} %copy.7, bf16[4,8,2048]{1,0,2:T(4,128)(2,1)} %copy.14), kind=kOutput, calls=%fused_computation.49 | convolution fusion | flops 4194304 | bytes 2752512 | tf_op jit(solution)/shard_map/wsf,wrf->rsf/dot_general | solution.py:40
  243.4 6.6 %copy.15 = f32[2048,32,8]{0,2,1:T(8,128)} copy(f32[2048,32,8]{1,2,0:T(8,128)} %fusion.41) | data formatting | bytes 4194304 | tf_op jit(solution)/shard_map/wsf,wrf->rsf/dot_general | solution.py:40
  250.0 7.2 %fusion.43 = f32[2048,32,8]{1,2,0:T(8,128)} fusion(bf16[4,32,2048]{1,0,2:T(4,128)(2,1)} %copy.4, bf16[4,8,2048]{1,0,2:T(4,128)(2,1)} %copy.14), kind=kOutput, calls=%fused_computation.51 | convolution fusion | flops 4194304 | bytes 2752512 | tf_op jit(solution)/shard_map/wsf,wrf->rsf/dot_general | solution.py:44
  257.2 6.7 %copy.17 = f32[2048,32,8]{0,2,1:T(8,128)} copy(f32[2048,32,8]{1,2,0:T(8,128)} %fusion.43) | data formatting | bytes 4194304 | tf_op jit(solution)/shard_map/wsf,wrf->rsf/dot_general | solution.py:44
  263.9 6.0 %fusion.42 = f32[2048,32,8]{1,2,0:T(8,128)} fusion(bf16[4,32,2048]{1,0,2:T(4,128)(2,1)S(1)} %copy.7, bf16[4,8,2048]{1,0,2:T(4,128)(2,1)} %copy.12), kind=kOutput, calls=%fused_computation.50 | convolution fusion | flops 4194304 | bytes 2752512 | tf_op jit(solution)/shard_map/wsf,wrf->rsf/dot_general | solution.py:43
  270.0 6.8 %copy.16 = f32[2048,32,8]{0,2,1:T(8,128)} copy(f32[2048,32,8]{1,2,0:T(8,128)} %fusion.42) | data formatting | bytes 4194304 | tf_op jit(solution)/shard_map/wsf,wrf->rsf/dot_general | solution.py:43
  276.8 2.0 add_bitcast_fusion
  279.9 2.4 pad_maximum_fusion.1
  282.4 18.0 %fusion.15 = (f32[2048,512]{1,0:T(8,128)}, f32[2048,512]{1,0:T(8,128)}) fusion(s32[512]{0:T(512)S(1)} %iota_add_fusion), kind=kLoop, calls=%fused_computation.24 | loop fusion | flops 15728640 | bytes 8390656 | tf_op jit(solution)/shard_map/cos | solution.py:22
  300.4 26.2 %reduce-scatter.3.cloned.1.call-done = f32[2,8,4096]{2,1,0:T(8,128)} async-done(((f32[32,8,4096]{2,1,0:T(8,128)}), f32[2,8,4096]{2,1,0:T(8,128)}) %reduce-scatter.3.cloned.1.call-update) | async-done | bytes 262160 | tf_op jit(solution)/shard_map/reduce_scatter | solution.py:75
  326.6 7.8 %fusion.25 = bf16[1,2,8,512]{3,2,1,0:T(8,128)(2,1)S(1)} fusion(f32[2,8,4096]{2,1,0:T(8,128)} %reduce-scatter.3.cloned.1.call-done, f32[2048,512]{1,0:T(8,128)} %get-tuple-element.16, f32[2048,512]{1,0:T(8,128)} %get-tuple-element.15), kind=kOutput, calls=%fused_computation.30 | convolution fusion | flops 406855680 | bytes 8667136 | tf_op jit(solution)/shard_map/dot_general | solution.py:51
  334.4 94.7 %reduce-scatter.5.cloned.1.call-done = f32[2,8,4096]{2,1,0:T(8,128)} async-done(((f32[32,8,4096]{2,1,0:T(8,128)}), f32[2,8,4096]{2,1,0:T(8,128)}) %reduce-scatter.5.cloned.1.call-update) | async-done | bytes 262160 | tf_op jit(solution)/shard_map/reduce_scatter | solution.py:75
  429.1 7.8 %fusion.22 = bf16[1,2,8,512]{3,2,1,0:T(8,128)(2,1)S(1)} fusion(f32[2,8,4096]{2,1,0:T(8,128)} %reduce-scatter.5.cloned.1.call-done, f32[2048,512]{1,0:T(8,128)} %get-tuple-element.16, f32[2048,512]{1,0:T(8,128)} %get-tuple-element.15), kind=kOutput, calls=%fused_computation.29 | convolution fusion | flops 406855680 | bytes 8667136 | tf_op jit(solution)/shard_map/dot_general | solution.py:51
  (34 shorter events, 10.1 us)
Async XLA Ops:
  6.5 151.4 %all-reduce.3.cloned.1.call-start = ((), (), s32[]{:S(2)}) async-start(), calls=%async_computation.4 | async-start | bytes 1048576 | tf_op jit(solution)/shard_map/psum | solution.py:14
  17.7 308.9 %reduce-scatter.3.cloned.1.call-start = ((), (), s32[]{:S(2)}) async-start(), calls=%async_computation.2 | async-start | bytes 4456448 | tf_op jit(solution)/shard_map/reduce_scatter | solution.py:75
  163.9 7.4 %copy-start.2 = (bf16[4,8,2048]{1,0,2:T(4,128)(2,1)S(1)}, bf16[4,8,2048]{1,0,2:T(4,128)(2,1)}, u32[]{:S(2)}) copy-start(bf16[4,8,2048]{1,0,2:T(4,128)(2,1)} %copy.5) | copy-start | bytes 393220
  171.3 4.8 %copy-start.1 = (bf16[4,8,2048]{1,0,2:T(4,128)(2,1)S(1)}, bf16[4,8,2048]{1,0,2:T(4,128)(2,1)}, u32[]{:S(2)}) copy-start(bf16[4,8,2048]{1,0,2:T(4,128)(2,1)} %copy.8) | copy-start | bytes 393220
  176.1 4.8 %copy-start = (bf16[4,32,2048]{1,0,2:T(4,128)(2,1)S(1)}, bf16[4,32,2048]{1,0,2:T(4,128)(2,1)}, u32[]{:S(2)}) copy-start(bf16[4,32,2048]{1,0,2:T(4,128)(2,1)} %copy.4) | copy-start | bytes 1572868
  212.2 2.9 copy-start.5
  212.2 3.5 copy-start.6
  218.4 210.7 %reduce-scatter.5.cloned.1.call-start = ((), (), s32[]{:S(2)}) async-start(), calls=%async_computation.3 | async-start | bytes 4456448 | tf_op jit(solution)/shard_map/reduce_scatter | solution.py:75
  270.0 6.8 %copy-start.3 = (f32[2048,32,8]{0,2,1:T(8,128)S(1)}, f32[2048,32,8]{0,2,1:T(8,128)}, u32[]{:S(2)}) copy-start(f32[2048,32,8]{0,2,1:T(8,128)} %copy.13) | copy-start | bytes 6291460
  276.8 2.2 copy-start.4
  276.8 2.9 copy-start.7
Sparse Core Ops, SparseCore 0:
  17.8 140.0 all-reduce.2
  218.5 108.0 reduce-scatter.2
  329.3 99.7 reduce-scatter.4
where the time goes:
time: 445 us; the launch traced here: 444 us
  waiting for transfers between devices  257 us (58%)
  local copies, waits for them, and re-layouts  71.1 us (16%)
  matrix products  63.9 us (14%)
  other arithmetic  33.3 us (7%)
  between operations  18.4 us (4%)
    psum x1, waiting for transfers between devices, from_root(): return lax.psum(kept, axis)  136 us
    reduce_scatter x2, waiting for transfers between devices, body(): lax.psum_scatter(partial_cross, 'win', scatter_dimension=0, tiled=True)  121 us
    cos x1, other arithmetic, lag_table(): jnp.cos(phase_angle)  18 us
    dot_general x2, matrix products, apply_lags(): jnp.dot(cross.reshape(-1, cross.shape[-1]), transform, precision=lax.Prec...  15.6 us
    dot_general x2, matrix products, cross_spectra(): jnp.einsum('wsf,wrf->rsf', src_real, rec_real, preferred_element_type=jnp...  14.6 us
    dot_general x2, local copies, waits for them, and re-layouts, cross_spectra(): jnp.einsum('wsf,wrf->rsf', src_real, rec_imag, preferred_element_type=jnp...  13.5 us
    dot_general x2, local copies, waits for them, and re-layouts, cross_spectra(): jnp.einsum('wsf,wrf->rsf', src_real, rec_real, preferred_element_type=jnp...  13.3 us
    dot_general x2, local copies, waits for them, and re-layouts, cross_spectra(): jnp.einsum('wsf,wrf->rsf', src_imag, rec_real, preferred_element_type=jnp...  13.3 us
  transfers between devices with their start and end apart: 3, of which 3 were waited for; matrix products, arithmetic and copies ran while one was open for 21% of the time, Pallas kernels for 0%

commit v1 on v0

--- a/solution.py
+++ b/solution.py
@@ -11,7 +11,8 @@
 
 def from_root(value, axis, source):
     kept = jnp.where(lax.axis_index(axis) == source, value, 0).astype(value.dtype)
-    return lax.psum(kept, axis)
+    deliver_forms_on_mesh = lambda inputs, across: jnp.sum(lax.all_gather(inputs, across), axis=0)
+    return deliver_forms_on_mesh(kept, axis)
 
 
 def lag_table(bins, lags, factor):

time: 445 us -> 365 us (0.82)
  waiting for transfers between devices: 257 us -> 166 us
  other arithmetic: 33.3 us -> 41.6 us
  matrix products: 63.9 us -> 68.8 us
    psum x1 -> x0, waiting for transfers between devices: 136 us -> none  [from_root(): return lax.psum(kept, axis)]
    all_gather x0 -> x2, waiting for transfers between devices: none -> 57.3 us  [from_root(): lax.all_gather(inputs, across)]
    reduce_scatter x2, waiting for transfers between devices: 121 us -> 108 us  [body(): lax.psum_scatter(partial_cross, 'win', scatter_dimension=0, tiled=True)]
    sub x2, other arithmetic: 0.5 us -> 7.87 us  [cross_spectra(): imag_part - jnp.einsum('wsf,wrf->rsf', src_imag, rec_real, preferred_elem...]
    reduce_sum x0 -> x2, other arithmetic: none -> 5.97 us  [from_root(): jnp.sum(lax.all_gather(inputs, across), axis=0)]
    add x2 -> x0, other arithmetic: 4.68 us -> none  [cross_spectra(): real_part + jnp.einsum('wsf,wrf->rsf', src_imag, rec_imag, preferred_elem...]
  transfers between devices with their start and end apart: 3 -> 4, of which waited for: 3 -> 3; matrix products, arithmetic and copies ran while one was open for 21% -> 45% of each run, Pallas kernels for 0% -> 0%
where the time goes in v1:
time: 365 us; the launch traced here: 364 us
  waiting for transfers between devices  166 us (45%)
  matrix products  68.8 us (19%)
  local copies, waits for them, and re-layouts  68.7 us (19%)
  other arithmetic  41.6 us (11%)
  between operations  18.6 us (5%)
    reduce_scatter x2, waiting for transfers between devices, body(): lax.psum_scatter(partial_cross, 'win', scatter_dimension=0, tiled=True)  108 us
    all_gather x2, waiting for transfers between devices, from_root(): lax.all_gather(inputs, across)  57.3 us
    cos x1, other arithmetic, lag_table(): jnp.cos(phase_angle)  18 us
    dot_general x2, matrix products, apply_lags(): jnp.dot(cross.reshape(-1, cross.shape[-1]), transform, precision=lax.Prec...  15.6 us
    dot_general x2, matrix products, cross_spectra(): jnp.einsum('wsf,wrf->rsf', src_imag, rec_real, preferred_element_type=jnp...  14.6 us
    dot_general x2, matrix products, cross_spectra(): jnp.einsum('wsf,wrf->rsf', src_real, rec_real, preferred_element_type=jnp...  14.5 us
    dot_general x2, local copies, waits for them, and re-layouts, cross_spectra(): jnp.einsum('wsf,wrf->rsf', src_real, rec_imag, preferred_element_type=jnp...  13.5 us
    dot_general x2, local copies, waits for them, and re-layouts, cross_spectra(): jnp.einsum('wsf,wrf->rsf', src_imag, rec_imag, preferred_element_type=jnp...  13.4 us
  transfers between devices with their start and end apart: 4, of which 3 were waited for; matrix products, arithmetic and copies ran while one was open for 45% of the time, Pallas kernels for 0%

profile of v1, /device:TPU:8, one launch (start us, length us, event | category | flops | bytes accessed | tf_op | source)
XLA Modules:
  0.0 364.2 jit_solution(15475940115260367823)
XLA Ops:
  20.2 2.5 copy.4
  22.7 57.3 %all-gather.5.cloned.1.call-done = bf16[64,8,4096]{2,1,0:T(8,128)(2,1)} async-done(((bf16[4,8,4096]{2,1,0:T(8,128)(2,1)}), bf16[64,8,4096]{2,1,0:T(8,128)(2,1)}) %all-gather.5.cloned.1.call-update) | async-done | bytes 4194320 | tf_op jit(solution)/shard_map/all_gather | solution.py:14
  80.0 3.0 reduce_sum.34
  83.0 2.4 copy.5
  85.5 6.0 %fusion.38 = f32[2048,32,8]{1,2,0:T(8,128)} fusion(bf16[4,32,2048]{1,0,2:T(4,128)(2,1)S(1)} %copy.7, bf16[4,8,2048]{1,0,2:T(4,128)(2,1)} %copy.5), kind=kOutput, calls=%fused_computation.46 | convolution fusion | flops 4194304 | bytes 2752512 | tf_op jit(solution)/shard_map/wsf,wrf->rsf/dot_general | solution.py:44
  91.5 6.7 %copy.10 = f32[2048,32,8]{0,2,1:T(8,128)} copy(f32[2048,32,8]{1,2,0:T(8,128)} %fusion.38) | data formatting | bytes 4194304 | tf_op jit(solution)/shard_map/wsf,wrf->rsf/dot_general | solution.py:44
  98.2 2.4 copy.8
  100.6 7.3 %fusion.39 = f32[2048,32,8]{1,2,0:T(8,128)} fusion(bf16[4,32,2048]{1,0,2:T(4,128)(2,1)} %copy.4, bf16[4,8,2048]{1,0,2:T(4,128)(2,1)} %copy.8), kind=kOutput, calls=%fused_computation.47 | convolution fusion | flops 4194304 | bytes 2752512 | tf_op jit(solution)/shard_map/wsf,wrf->rsf/dot_general | solution.py:45
  107.9 6.6 %copy.11 = f32[2048,32,8]{0,2,1:T(8,128)} copy(f32[2048,32,8]{1,2,0:T(8,128)} %fusion.39) | data formatting | bytes 4194304 | tf_op jit(solution)/shard_map/wsf,wrf->rsf/dot_general | solution.py:45
  114.5 7.2 %fusion.36 = f32[2048,32,8]{1,2,0:T(8,128)} fusion(bf16[4,32,2048]{1,0,2:T(4,128)(2,1)} %copy.4, bf16[4,8,2048]{1,0,2:T(4,128)(2,1)} %copy.5), kind=kOutput, calls=%fused_computation.44 | convolution fusion | flops 4194304 | bytes 2752512 | tf_op jit(solution)/shard_map/wsf,wrf->rsf/dot_general | solution.py:40
  121.8 6.6 %copy.6 = f32[2048,32,8]{0,2,1:T(8,128)} copy(f32[2048,32,8]{1,2,0:T(8,128)} %fusion.36) | data formatting | bytes 4194304 | tf_op jit(solution)/shard_map/wsf,wrf->rsf/dot_general | solution.py:40
  128.4 6.0 %fusion.37 = f32[2048,32,8]{1,2,0:T(8,128)} fusion(bf16[4,32,2048]{1,0,2:T(4,128)(2,1)S(1)} %copy.7, bf16[4,8,2048]{1,0,2:T(4,128)(2,1)} %copy.8), kind=kOutput, calls=%fused_computation.45 | convolution fusion | flops 4194304 | bytes 2752512 | tf_op jit(solution)/shard_map/wsf,wrf->rsf/dot_general | solution.py:41
  134.5 6.8 %copy.9 = f32[2048,32,8]{0,2,1:T(8,128)} copy(f32[2048,32,8]{1,2,0:T(8,128)} %fusion.37) | data formatting | bytes 4194304 | tf_op jit(solution)/shard_map/wsf,wrf->rsf/dot_general | solution.py:41
  141.2 4.2 %subtract_bitcast_fusion.1 = (f32[32,8,2048]{2,1,0:T(8,128)S(1)}, f32[32,8,2048]{2,1,0:T(8,128)S(1)}) fusion(f32[2048,32,8]{0,2,1:T(8,128)} %copy.10, f32[2048,32,8]{0,2,1:T(8,128)} %copy.11, f32[2048,32,8]{0,2,1:T(8,128)} %copy.6, f32[2048,32,8]{0,2,1:T(8,128)} %copy.9), kind=kLoop, calls=%fused_computation.25 | loop fusion | flops 1048576 | bytes 12582912 | tf_op jit(solution)/shard_map/sub | solution.py:45
  145.5 2.3 pad_maximum_fusion
  148.0 3.0 reduce_sum.35
  151.0 2.5 copy.12
  153.5 7.2 %fusion.40 = f32[2048,32,8]{1,2,0:T(8,128)} fusion(bf16[4,32,2048]{1,0,2:T(4,128)(2,1)} %copy.4, bf16[4,8,2048]{1,0,2:T(4,128)(2,1)} %copy.12), kind=kOutput, calls=%fused_computation.48 | convolution fusion | flops 4194304 | bytes 2752512 | tf_op jit(solution)/shard_map/wsf,wrf->rsf/dot_general | solution.py:40
  160.7 6.6 %copy.13 = f32[2048,32,8]{0,2,1:T(8,128)} copy(f32[2048,32,8]{1,2,0:T(8,128)} %fusion.40) | data formatting | bytes 4194304 | tf_op jit(solution)/shard_map/wsf,wrf->rsf/dot_general | solution.py:40
  167.4 2.4 copy.14
  169.8 6.1 %fusion.41 = f32[2048,32,8]{1,2,0:T(8,128)} fusion(bf16[4,32,2048]{1,0,2:T(4,128)(2,1)S(1)} %copy.7, bf16[4,8,2048]{1,0,2:T(4,128)(2,1)} %copy.14), kind=kOutput, calls=%fused_computation.49 | convolution fusion | flops 4194304 | bytes 2752512 | tf_op jit(solution)/shard_map/wsf,wrf->rsf/dot_general | solution.py:41
  175.9 6.7 %copy.15 = f32[2048,32,8]{0,2,1:T(8,128)} copy(f32[2048,32,8]{1,2,0:T(8,128)} %fusion.41) | data formatting | bytes 4194304 | tf_op jit(solution)/shard_map/wsf,wrf->rsf/dot_general | solution.py:41
  182.5 7.3 %fusion.43 = f32[2048,32,8]{1,2,0:T(8,128)} fusion(bf16[4,32,2048]{1,0,2:T(4,128)(2,1)} %copy.4, bf16[4,8,2048]{1,0,2:T(4,128)(2,1)} %copy.14), kind=kOutput, calls=%fused_computation.51 | convolution fusion | flops 4194304 | bytes 2752512 | tf_op jit(solution)/shard_map/wsf,wrf->rsf/dot_general | solution.py:45
  189.8 6.7 %copy.17 = f32[2048,32,8]{0,2,1:T(8,128)} copy(f32[2048,32,8]{1,2,0:T(8,128)} %fusion.43) | data formatting | bytes 4194304 | tf_op jit(solution)/shard_map/wsf,wrf->rsf/dot_general | solution.py:45
  196.5 6.1 %fusion.42 = f32[2048,32,8]{1,2,0:T(8,128)} fusion(bf16[4,32,2048]{1,0,2:T(4,128)(2,1)S(1)} %copy.7, bf16[4,8,2048]{1,0,2:T(4,128)(2,1)} %copy.12), kind=kOutput, calls=%fused_computation.50 | convolution fusion | flops 4194304 | bytes 2752512 | tf_op jit(solution)/shard_map/wsf,wrf->rsf/dot_general | solution.py:44
  202.5 6.8 %copy.16 = f32[2048,32,8]{0,2,1:T(8,128)} copy(f32[2048,32,8]{1,2,0:T(8,128)} %fusion.42) | data formatting | bytes 4194304 | tf_op jit(solution)/shard_map/wsf,wrf->rsf/dot_general | solution.py:44
  209.3 3.6 %subtract_bitcast_fusion = (f32[32,8,2048]{2,1,0:T(8,128)S(1)}, f32[32,8,2048]{2,1,0:T(8,128)S(1)}) fusion(f32[2048,32,8]{0,2,1:T(8,128)} %copy.16, f32[2048,32,8]{0,2,1:T(8,128)} %copy.17, f32[2048,32,8]{0,2,1:T(8,128)S(1)} %copy-done, f32[2048,32,8]{0,2,1:T(8,128)} %copy.15), kind=kLoop, calls=%fused_computation.22 | loop fusion | flops 1048576 | bytes 12582912 | tf_op jit(solution)/shard_map/sub | solution.py:45
  215.3 18.0 %fusion.15 = (f32[2048,512]{1,0:T(8,128)}, f32[2048,512]{1,0:T(8,128)}) fusion(s32[512]{0:T(512)S(1)} %iota_add_fusion), kind=kLoop, calls=%fused_computation.24 | loop fusion | flops 15728640 | bytes 8390656 | tf_op jit(solution)/shard_map/cos | solution.py:23
  233.3 13.9 %reduce-scatter.3.cloned.1.call-done = f32[2,8,4096]{2,1,0:T(8,128)} async-done(((f32[32,8,4096]{2,1,0:T(8,128)}), f32[2,8,4096]{2,1,0:T(8,128)}) %reduce-scatter.3.cloned.1.call-update) | async-done | bytes 262160 | tf_op jit(solution)/shard_map/reduce_scatter | solution.py:76
  247.2 7.8 %fusion.25 = bf16[1,2,8,512]{3,2,1,0:T(8,128)(2,1)S(1)} fusion(f32[2,8,4096]{2,1,0:T(8,128)} %reduce-scatter.3.cloned.1.call-done, f32[2048,512]{1,0:T(8,128)} %get-tuple-element.14, f32[2048,512]{1,0:T(8,128)} %get-tuple-element.13), kind=kOutput, calls=%fused_computation.30 | convolution fusion | flops 406855680 | bytes 8667136 | tf_op jit(solution)/shard_map/dot_general | solution.py:52
  255.0 94.3 %reduce-scatter.5.cloned.1.call-done = f32[2,8,4096]{2,1,0:T(8,128)} async-done(((f32[32,8,4096]{2,1,0:T(8,128)}), f32[2,8,4096]{2,1,0:T(8,128)}) %reduce-scatter.5.cloned.1.call-update) | async-done | bytes 262160 | tf_op jit(solution)/shard_map/reduce_scatter | solution.py:76
  349.3 7.8 %fusion.22 = bf16[1,2,8,512]{3,2,1,0:T(8,128)(2,1)S(1)} fusion(f32[2,8,4096]{2,1,0:T(8,128)} %reduce-scatter.5.cloned.1.call-done, f32[2048,512]{1,0:T(8,128)} %get-tuple-element.14, f32[2048,512]{1,0:T(8,128)} %get-tuple-element.13), kind=kOutput, calls=%fused_computation.29 | convolution fusion | flops 406855680 | bytes 8667136 | tf_op jit(solution)/shard_map/dot_general | solution.py:52
  (24 shorter events, 11.4 us)
Async XLA Ops:
  6.5 73.5 %all-gather.5.cloned.1.call-start = ((), (), s32[]{:S(2)}) async-start(), calls=%async_computation.4 | async-start | bytes 4456448 | tf_op jit(solution)/shard_map/all_gather | solution.py:14
  17.9 130.1 %all-gather.7.cloned.1.call-start = ((), (), s32[]{:S(2)}) async-start(), calls=%async_computation.5 | async-start | bytes 4456448 | tf_op jit(solution)/shard_map/all_gather | solution.py:14
  18.7 228.5 %reduce-scatter.3.cloned.1.call-start = ((), (), s32[]{:S(2)}) async-start(), calls=%async_computation.2 | async-start | bytes 4456448 | tf_op jit(solution)/shard_map/reduce_scatter | solution.py:76
  147.8 201.5 %reduce-scatter.5.cloned.1.call-start = ((), (), s32[]{:S(2)}) async-start(), calls=%async_computation.3 | async-start | bytes 4456448 | tf_op jit(solution)/shard_map/reduce_scatter | solution.py:76
  202.5 6.8 %copy-start = (f32[2048,32,8]{0,2,1:T(8,128)S(1)}, f32[2048,32,8]{0,2,1:T(8,128)}, u32[]{:S(2)}) copy-start(f32[2048,32,8]{0,2,1:T(8,128)} %copy.13) | copy-start | bytes 6291460
Sparse Core Ops, SparseCore 0:
  18.1 61.9 all-gather.4
  82.8 58.2 all-gather.6
  147.9 99.2 reduce-scatter.2
  249.6 99.6 reduce-scatter.4
